TPU v7x, 32 devices: a whole 2x2x4 slice. The times are simulated.
32 devices in a mesh: row: 4 (over z), col: 8 (over y, x, core).
Axes of the slice: x: 2, y: 2, z: 4, core: 2. Of those that a mesh axis runs over, the one named last changes fastest.
Arguments:
- front: float32 [8192, 8192], P('row', 'col'), may hold values from -6 to 6
- inverses: float32 [2, 512, 512], replicated, may hold values from -2 to 2, as said below
- block_owner: int32 [64, 64], P('row', 'col'), may hold values from -1 to 31, as said below
- block_slot: int32 [64, 64], P('row', 'col'), may hold values from 0 to 47
- parent_in: float32 [1536, 128, 128], P(('row', 'col')), may hold values from -6 to 6
Outputs:
- updated: float32 [8192, 8192], P('row', 'col')
- panels: float32 [8192, 1024], P(('row', 'col'))
- parent_out: float32 [1536, 128, 128], P(('row', 'col'))
Inputs may be any that keep to these rules, and one draw needn't show every extreme that they name: Entries of the pivot block inverses. `block_owner`: -1 exactly for blocks above the diagonal (I < J); on one device's 16 x 8 blocks no device is named more than 4 times, and on some device some device is named exactly 4 times.
All inputs are finite; a program needn't handle non-finite values.
Results may differ from a plain program's by a relative error of at most 0.00014.
Values sent between devices are 32-bit elements; how exact they have to be, the bound alone decides.
A program may use at most 128 MiB of HBM per device.

v0:
```python
import functools

import jax
import jax.numpy as jnp
from jax import lax
from jax.experimental import pallas as pl
from jax.experimental.pallas import tpu as pltpu
from jax.sharding import PartitionSpec as P

MESH = pl.DeviceIdType.MESH
ANY = pl.BlockSpec(memory_space=pl.ANY)
VMEM = pl.BlockSpec(memory_space=pltpu.VMEM)
HBM = pl.BlockSpec(memory_space=pltpu.MemorySpace.HBM)
SMEM = pl.BlockSpec(memory_space=pltpu.SMEM)


def chip_paths(chips):
    order = [i ^ (i >> 1) for i in range(chips)]
    if sorted(order) != list(range(chips)):
        order = list(range(chips))
    return order, [order[0]] + order[1:][::-1]


def pick(value, pairs, default):
    out = jnp.int32(default)
    for key, result in pairs:
        out = jnp.where(value == key, jnp.int32(result), out)
    return out


STEPS = 8
FINE = 2
LAG = 4


def split3(value, axis):
    high = value.astype(jnp.bfloat16)
    low = (value - high.astype(jnp.float32)).astype(jnp.bfloat16)
    return high, low


def front_kernel(
    nrow, ncol, width, cap, brows, bcols, bits,
    packed, front, inverses,
    acc, panels, arrived, marks,
    cut, lbuf, ubuf, ustack, inv, istack, blocks,
    chain_send, side_send, half_recv, row_send, row_recv,
    table, label_rows, labels, where, load_sem, misc_sem, send, recv, mid_recv, label_send, label_recv, gate,
):
    row = lax.axis_index("row")
    col = lax.axis_index("col")
    n = nrow * ncol
    me = row * ncol + col
    chips = ncol // 2
    chip = col // 2
    core = col % 2
    paths = chip_paths(chips)
    nk, rows_all, kc = lbuf.shape
    cols_all = acc.shape[1]
    edge = blocks.shape[1]
    half = rows_all // 2
    ts = half // STEPS
    us = kc // STEPS
    shift = width // ts
    mid = nk // 2
    nexts = [pick(chip, list(zip(p[:-1], p[1:])), 0) for p in paths]
    places = [pick(chip, [(c, at) for at, c in enumerate(p)], 0) for p in paths]
    total = nk * STEPS
    fine = total * FINE
    ls = ts // FINE
    us = us // FINE

    def tile_rows(h, tile):
        return pl.ds(pl.multiple_of(h * half + tile * ts, ts), ts)

    def l_copy(h, t, send_sem, target):
        tile = (t // FINE % STEPS + shift) % STEPS
        first = pl.multiple_of(h * half + tile * ts + t % FINE * ls, ls)
        at = lbuf.at[t // FINE // STEPS, pl.ds(first, ls), :]
        return pltpu.make_async_remote_copy(
            src_ref=at, dst_ref=at,
            send_sem=send_sem.at[h, t], recv_sem=half_recv.at[h, t],
            device_id=(row, target), device_id_type=MESH,
        )

    def u_copy(src, t):
        s = pl.ds(pl.multiple_of(t * us, us), us)
        return pltpu.make_async_remote_copy(
            src_ref=src.at[s, :], dst_ref=ubuf.at[s, :],
            send_sem=row_send.at[t], recv_sem=row_recv.at[t],
            device_id=(row + 1, col), device_id_type=MESH,
        )

    def load(h, i):
        s = tile_rows(h, (i + shift) % STEPS)
        return pltpu.make_async_copy(front.at[s, :], acc.at[s, :], load_sem.at[h, i])

    def load_inv(p):
        return pltpu.make_async_copy(inverses.at[p], inv, misc_sem.at[0])

    load_rows = pltpu.make_async_copy(
        front.at[pl.ds(0, width), :], ubuf.at[pl.ds(0, width), :], misc_sem.at[1]
    )
    piece = rows_all // ncol

    def panel_store(k):
        return pltpu.make_async_copy(
            lbuf.at[k, pl.ds(pl.multiple_of(col * piece, piece), piece), :],
            panels.at[:, pl.ds(k * kc, kc)], misc_sem.at[2 + k],
        )

    def active(r, c):
        return r * brows + brows - 1 >= c * bcols

    def part(index):
        return pl.ds(index * cap, cap)

    def straight(source, target):
        return pltpu.make_async_remote_copy(
            src_ref=blocks.at[part(target)], dst_ref=arrived.at[part(source)],
            send_sem=send.at[target], recv_sem=recv.at[source],
            device_id=(target // ncol, target % ncol), device_id_type=MESH,
        )

    def hop(to_row, to_col):
        target = to_row * ncol + to_col
        return pltpu.make_async_remote_copy(
            src_ref=blocks.at[part(target)], dst_ref=blocks.at[part(to_row * ncol + col)],
            send_sem=send.at[target], recv_sem=mid_recv.at[to_row * ncol + col],
            device_id=(row, to_col), device_id_type=MESH,
        )

    def landed(to_row, from_col):
        return pltpu.make_async_remote_copy(
            src_ref=blocks.at[part(0)], dst_ref=blocks.at[part(to_row * ncol + from_col)],
            send_sem=send.at[0], recv_sem=mid_recv.at[to_row * ncol + from_col],
            device_id=(row, from_col), device_id_type=MESH,
        )

    def relay(to_row, from_col):
        return pltpu.make_async_remote_copy(
            src_ref=blocks.at[part(to_row * ncol + from_col)],
            dst_ref=arrived.at[part(row * ncol + from_col)],
            send_sem=send.at[to_row * ncol + from_col],
            recv_sem=recv.at[row * ncol + from_col],
            device_id=(to_row, col), device_id_type=MESH,
        )

    def label_copy(source, target):
        return pltpu.make_async_remote_copy(
            src_ref=labels.at[target], dst_ref=marks.at[source],
            send_sem=label_send.at[target], recv_sem=label_recv.at[source],
            device_id=(target // ncol, target % ncol), device_id_type=MESH,
        )

    own_blocks = pltpu.make_async_copy(
        blocks.at[part(me)], arrived.at[part(me)], misc_sem.at[2 + nk]
    )
    own_labels = pltpu.make_async_copy(labels.at[me], marks.at[me], misc_sem.at[3 + nk])

    def local_loads():
        @pl.when(col == 0)
        def _():
            load_inv(0).start()

        def start_load(i, carry):
            for h in range(2):
                load(h, i).start()
            return carry

        lax.fori_loop(0, STEPS, start_load, 0)

        @pl.when(row == 0)
        def _():
            load_rows.start()

    barrier = pltpu.get_barrier_semaphore()

    def greet(d, carry):
        other = (me + d) % n
        pl.semaphore_signal(
            barrier, 1, device_id=(other // ncol, other % ncol), device_id_type=MESH
        )
        return carry

    def make_tables():
        count = brows * bcols
        owner = packed[...] >> bits
        slot = (packed[...] & ((1 << bits) - 1)).astype(jnp.float32)
        hit = owner == lax.broadcasted_iota(jnp.int32, (n, count), 0)
        before = lax.broadcasted_iota(jnp.int32, (count, count), 0) < (
            lax.broadcasted_iota(jnp.int32, (count, count), 1)
        )
        rank = jnp.dot(
            jnp.where(hit, 1.0, 0.0), jnp.where(before, 1.0, 0.0),
            preferred_element_type=jnp.float32,
        )
        position = lax.broadcasted_iota(jnp.int32, (n, count), 1).astype(jnp.float32)
        lane = lax.broadcasted_iota(jnp.int32, (n, 128), 1)
        spots = jnp.zeros((n, 128), jnp.float32)
        names = jnp.full((n, 128), -1.0, jnp.float32)
        for q in range(cap):
            chosen = hit & (rank == q)
            spot = jnp.sum(jnp.where(chosen, position, 0.0), axis=1, keepdims=True)
            name = jnp.sum(jnp.where(chosen, slot + 1.0, 0.0), axis=1, keepdims=True) - 1.0
            spots = jnp.where(lane == q, spot, spots)
            names = jnp.where(lane == q, name, names)
        table[...] = spots.astype(jnp.int32)
        label_rows[...] = names.astype(jnp.int32)

        def spread_label(d, carry):
            labels[d] = jnp.broadcast_to(label_rows[pl.ds(d, 1), :], labels.shape[1:])
            return carry

        lax.fori_loop(0, n, spread_label, 0)

    lax.fori_loop(1, n, greet, 0)
    local_loads()
    make_tables()
    pl.semaphore_wait(barrier, n - 1)
    load_table = pltpu.make_async_copy(table, where, misc_sem.at[4 + nk])
    load_table.start()

    @pl.when(core == 1)
    def _():
        def early(u, carry):
            for h in range(2):
                t = u - LAG * jnp.maximum(places[h] - 1, 0)

                @pl.when((t >= 0) & (t < fine))
                def _(h=h, t=t):
                    l_copy(h, t, chain_send, 0).wait_recv()
                    if chips > 1:
                        @pl.when(places[h] < chips - 1)
                        def _():
                            l_copy(h, t, chain_send, nexts[h] * 2 + 1).start()

                    @pl.when(chip > 0)
                    def _():
                        l_copy(h, t, side_send, chip * 2).start()

            return carry

        lax.fori_loop(0, fine + LAG * max(chips - 2, 0), early, 0)

    def stacked(value):
        high, low = split3(value, 1)
        return jnp.concatenate([high, high, low], axis=1)

    def split_rows(source, target, depth):
        high, low = split3(source, 0)
        target[pl.ds(0, depth), :] = high
        target[pl.ds(depth, depth), :] = low
        target[pl.ds(2 * depth, depth), :] = high

    def update(k, i):
        @pl.when(i == 0)
        def _():
            for q in range(cols_all // edge // 2):
                s = pl.ds(q * 2 * edge, 2 * edge)
                split_rows(
                    ubuf[pl.ds(pl.multiple_of(k * kc, kc), kc), s], ustack.at[:, s], kc
                )

        t = k * STEPS + i
        tile = (i + shift) % STEPS

        @pl.when((core == 0) & (col > 0))
        def _():
            for h in range(2):
                for g in range(FINE):
                    l_copy(h, t * FINE + g, chain_send, 0).wait_recv()

        both = jnp.concatenate([lbuf[k, tile_rows(h, tile), :] for h in range(2)], axis=0)
        a = stacked(both)
        for q in range(cols_all // edge // 2):
            s = pl.ds(q * 2 * edge, 2 * edge)
            out = jnp.dot(a, ustack[:, s], preferred_element_type=jnp.float32)
            for h in range(2):
                at = tile_rows(h, tile)
                acc[at, s] = acc[at, s] - out[h * ts:(h + 1) * ts]

        @pl.when(k == nk - 1)
        def _():
            for h in range(2):
                for u in range(ts // edge):
                    at = pl.ds(pl.multiple_of(h * half + tile * ts + u * edge, edge), edge)
                    first = ((h * STEPS + tile) * (ts // edge) + u) * bcols
                    for q in range(bcols):
                        cut[first + q] = acc[at, pl.ds(q * edge, edge)]

        @pl.when((row == 0) & (k == mid - 1) & (i < width // ts))
        def _():
            at = tile_rows(0, tile)
            ubuf[at, :] = acc[at, :]

    def produce(p, i):
        @pl.when(i == 0)
        def _():
            load_inv(p).wait()
            for q in range(width // 256):
                s = pl.ds(q * 256, 256)
                split_rows(inv[:, s], istack.at[:, s], width)

            @pl.when(p == 0)
            def _():
                load_inv(1).start()

        tile = (i + shift) % STEPS
        from_col = pl.ds(pl.multiple_of(p * width, width), width)
        both = jnp.concatenate([acc[tile_rows(h, tile), from_col] for h in range(2)], axis=0)
        a = stacked(both)
        for q in range(mid):
            out = jnp.dot(
                a, istack[:, pl.ds(q * kc, kc)], preferred_element_type=jnp.float32
            )
            for h in range(2):
                lbuf[p * mid + q, tile_rows(h, tile), :] = out[h * ts:(h + 1) * ts]

    def step(t, carry):
        k = t // STEPS
        i = t % STEPS

        @pl.when(k == 0)
        def _():
            for h in range(2):
                load(h, i).wait()

        @pl.when((row == 0) & (t == 0))
        def _():
            load_rows.wait()

        @pl.when(k > 0)
        def _():
            update(k - 1, i)

        @pl.when((col == 0) & ((k == 0) | (k == mid)))
        def _():
            produce(k // mid, i)

        @pl.when(k < nk)
        def _():
            @pl.when(col == 0)
            def _():
                for g in range(FINE):
                    for h in range(2):
                        l_copy(h, t * FINE + g, side_send, 1).start()

            if nrow > 1:
                for g in range(FINE):
                    @pl.when(row > 0)
                    def _(g=g):
                        u_copy(ubuf, t * FINE + g).wait_recv()

                    @pl.when(row < nrow - 1)
                    def _(g=g):
                        u_copy(ubuf, t * FINE + g).start()

        if nrow > 1:
            @pl.when((t == total) & (row < nrow - 1) & ((row == 0) | (core == 1)))
            def _():
                def sent(u, carry):
                    u_copy(ubuf, u).wait_send()
                    return carry

                lax.fori_loop(0, fine, sent, 0)
                pl.semaphore_signal(
                    gate, 1, device_id=(row, col + 1 - 2 * core), device_id_type=MESH
                )

        return carry

    if nrow > 1:
        @pl.when((row == 0) & (core == 1))
        def _():
            pl.semaphore_wait(gate, 1)

    lax.fori_loop(0, total + STEPS, step, 0)

    for k in range(nk):
        panel_store(k).start()

    load_table.wait()
    order = [(nrow // 2 + i) % nrow for i in range(nrow)]

    @pl.when(active(row, col))
    def _():
        def take(to_row, to_col):
            target = to_row * ncol + to_col
            for q in range(cap):
                spot = jnp.clip(where[target, q], 0, cut.shape[0] - 1)
                blocks[target * cap + q] = cut[spot]

        def give(to_row, to_col):
            target = to_row * ncol + to_col
            direct = active(row, to_col) | (to_row == row)

            @pl.when((target != me) & direct)
            def _():
                straight(me, target).start()

            @pl.when(jnp.logical_not(direct))
            def _():
                hop(to_row, to_col).start()

        def pieces(lift):
            def both(j, carry):
                to_col = (col + j) % ncol
                for o in order:
                    to_row = (row + o) % nrow

                    @pl.when((to_row > row) == lift)
                    def _(to_row=to_row):
                        give(to_row, to_col)

                return carry

            lax.fori_loop(0, ncol, both, 0)

        def fill(j, carry):
            to_col = (col + j) % ncol
            for o in order:
                take((row + o) % nrow, to_col)

                @pl.when(j > 0)
                def _(o=o):
                    to_row = (row + o) % nrow

                    @pl.when(to_row <= row)
                    def _():
                        give(to_row, (to_col + ncol - 1) % ncol)

            return carry

        lax.fori_loop(0, ncol, fill, 0)
        for o in order:
            @pl.when((row + o) % nrow <= row)
            def _(o=o):
                give((row + o) % nrow, (col + ncol - 1) % ncol)

        if nrow > 1:
            @pl.when((core == 0) & (row < nrow - 1))
            def _():
                pl.semaphore_wait(gate, 1)

        pieces(True)

        def label_step(d, carry):
            label_copy(me, (me + d) % n).start()
            return carry

        lax.fori_loop(1, n, label_step, 0)
        own_blocks.start()
        own_labels.start()

    def pass_on(act, lift):
        def body(j, carry):
            from_col = 2 * j % ncol + 2 * j // ncol

            @pl.when(active(row, from_col))
            def _():
                for o in order:
                    to_row = (row + o) % nrow

                    @pl.when((to_row != row) & ((to_row > row) == lift))
                    def _(to_row=to_row):
                        act(to_row, from_col)

            return carry

        @pl.when(jnp.logical_not(active(row, col)))
        def _():
            lax.fori_loop(0, ncol, body, 0)

    def forward(to_row, from_col):
        landed(to_row, from_col).wait_recv()
        relay(to_row, from_col).start()

    pass_on(forward, False)
    if nrow > 1:
        @pl.when((core == 0) & (row < nrow - 1) & jnp.logical_not(active(row, col)))
        def _():
            pl.semaphore_wait(gate, 1)

    pass_on(forward, True)

    def drain_l(t, carry):
        for h in range(2):
            @pl.when((col == 0) | ((core == 1) & (chip > 0)))
            def _(h=h):
                l_copy(h, t, side_send, 0).wait_send()

            if chips > 1:
                @pl.when((core == 1) & (places[h] < chips - 1))
                def _(h=h):
                    l_copy(h, t, chain_send, 0).wait_send()

        if nrow > 1:
            @pl.when((row < nrow - 1) & (row > 0) & (core == 0))
            def _():
                u_copy(ubuf, t).wait_send()

        return carry

    lax.fori_loop(0, fine, drain_l, 0)

    for k in range(nk):
        panel_store(k).wait()

    def arrive(s, carry):
        @pl.when((s != me) & active(s // ncol, s % ncol))
        def _():
            label_copy(s, 0).wait_recv()
            straight(s, 0).wait_recv()

        return carry

    lax.fori_loop(0, n, arrive, 0)

    @pl.when(active(row, col))
    def _():
        def drain(d, carry):
            target = (me + d) % n
            label_copy(me, target).wait_send()
            straight(me, target).wait_send()
            return carry

        lax.fori_loop(1, n, drain, 0)
        own_blocks.wait()
        own_labels.wait()

    for lift in (False, True):
        pass_on(lambda to_row, from_col: relay(to_row, from_col).wait_send(), lift)


def front_update(packed, front, inverses, brows, bcols, bits, cap, edge):
    nrow, ncol = lax.axis_size("row"), lax.axis_size("col")
    n = nrow * ncol
    width = inverses.shape[1]
    rows_all, cols_all = front.shape
    kc = width // 2
    nk = 4
    dma = pltpu.SemaphoreType.DMA
    f32, bf16 = jnp.float32, jnp.bfloat16
    shape = jax.ShapeDtypeStruct
    return pl.pallas_call(
        functools.partial(front_kernel, nrow, ncol, width, cap, brows, bcols, bits),
        out_shape=(
            shape(front.shape, f32),
            shape((rows_all // ncol, 2 * width), f32),
            shape((n * cap, edge, edge), f32),
            shape((n, 8, 128), jnp.int32),
        ),
        in_specs=[VMEM, ANY, ANY],
        out_specs=(VMEM, ANY, ANY, VMEM),
        scratch_shapes=[
            pltpu.VMEM((brows * bcols, edge, edge), f32),
            pltpu.VMEM((nk, rows_all, kc), f32),
            pltpu.VMEM((2 * width, cols_all), f32),
            pltpu.VMEM((3 * kc, cols_all), bf16),
            pltpu.VMEM((width, width), f32),
            pltpu.VMEM((3 * width, width), bf16),
            pltpu.VMEM((n * cap, edge, edge), f32),
            dma((2, nk * STEPS * FINE)), dma((2, nk * STEPS * FINE)),
            dma((2, nk * STEPS * FINE)),
            dma((nk * STEPS * FINE,)), dma((nk * STEPS * FINE,)),
            pltpu.VMEM((n, 128), jnp.int32),
            pltpu.VMEM((n, 128), jnp.int32),
            pltpu.VMEM((n, 8, 128), jnp.int32),
            pltpu.SMEM((n, 128), jnp.int32),
            dma((2, STEPS)), dma((5 + nk,)),
            dma((n,)), dma((n,)), dma((n,)), dma((n,)), dma((n,)),
            pltpu.SemaphoreType.REGULAR,
        ],
        compiler_params=pltpu.CompilerParams(
            has_side_effects=True, collective_id=0, vmem_limit_bytes=(34 << 20) + (n - 32) * (16 << 10)
        ),
        name="front_update",
    )(packed, front, inverses)


def add_kernel(
    ncol, brows, bcols, cap, names, parent, arrived, updated, panels,
    out, updated_out, panels_out, marks, parent_sem, name_sem, out_sem,
):
    n = arrived.shape[0] // cap
    parts = out_sem.shape[0] - 1
    rows = updated.shape[0] // parts

    def each(first, count, body):
        def step(s, carry):
            @pl.when(s // ncol * brows + brows - 1 >= s % ncol * bcols)
            def _():
                body(s)

            return carry

        lax.fori_loop(first, first + count, step, 0)

    def put(i):
        s = pl.ds(i * rows, rows)
        return pltpu.make_async_copy(updated.at[s, :], updated_out.at[s, :], out_sem.at[i])

    put_strip = pltpu.make_async_copy(panels, panels_out, out_sem.at[parts])
    whole = pltpu.make_async_copy(parent, out, parent_sem)
    load_names = pltpu.make_async_copy(names, marks, name_sem)
    load_names.start()
    whole.start()
    for i in range(parts):
        put(i).start()
    put_strip.start()
    load_names.wait()
    whole.wait()

    def add(s):
        for k in range(cap):
            m = marks[s, 0, k]

            @pl.when(m >= 0)
            def _(k=k, m=m):
                out[m] = out[m] + arrived[s * cap + k]

    each(0, n, add)
    for i in range(parts):
        put(i).wait()
    put_strip.wait()


def add_blocks(marks, parent, arrived, updated, panels, brows, bcols, cap):
    n = arrived.shape[0] // cap
    parts = 8
    like = lambda x: jax.ShapeDtypeStruct(x.shape, x.dtype)
    return pl.pallas_call(
        functools.partial(add_kernel, lax.axis_size("col"), brows, bcols, cap),
        out_shape=(like(parent), like(updated), like(panels)),
        in_specs=[ANY, VMEM, VMEM, VMEM, VMEM],
        out_specs=(VMEM, HBM, HBM),
        scratch_shapes=[
            pltpu.SMEM(marks.shape, marks.dtype),
            pltpu.SemaphoreType.DMA,
            pltpu.SemaphoreType.DMA,
            pltpu.SemaphoreType.DMA((parts + 1,)),
        ],
        compiler_params=pltpu.CompilerParams(vmem_limit_bytes=24<<20),
        name="add_blocks",
    )(marks, parent, arrived, updated, panels)


def local(front, inverses, block_owner, block_slot, parent_in):
    devices = lax.axis_size("row") * lax.axis_size("col")
    brows, bcols = block_owner.shape
    edge = parent_in.shape[1]
    count = brows * bcols
    cap = max(1, (count + devices - 1) // devices)
    bits = max(1, (parent_in.shape[0] - 1).bit_length())
    packed = ((block_owner << bits) + block_slot).reshape(1, count)
    updated, panels, arrived, marks = front_update(
        packed, front, inverses, brows, bcols, bits, cap, edge
    )
    parent_out, updated, panels = add_blocks(
        marks, parent_in, arrived, updated, panels, brows, bcols, cap
    )
    return (updated, panels, parent_out)


def solution(mesh):
    in_specs = (
        P("row", "col"),
        P(),
        P("row", "col"),
        P("row", "col"),
        P(("row", "col"), None, None),
    )
    out_specs = (P("row", "col"), P(("row", "col"), None), P(("row", "col"), None, None))
    return jax.shard_map(local, mesh=mesh, in_specs=in_specs, out_specs=out_specs, check_vma=False)
```

profile of v0, /device:TPU:15, one launch (start us, length us, event | category | flops | bytes accessed | tf_op | source)
XLA Modules:
  0.0 250.0 jit_solution(7406789564329887629)
XLA Ops:
  0.6 0.7 shift-left_add_fusion
  1.3 0.1 copy.9
  1.4 0.1 reshape.9.packed
  1.5 0.0 copy-start.1
  1.5 1.6 copy-done.1
  3.1 0.0 copy-start
  3.1 240.9 %front_update.1 = (f32[2048,1024]{1,0:T(8,128)S(1)}, f32[256,1024]{1,0:T(8,128)S(1)}, f32[128,128,128]{2,1,0:T(8,128)S(1)}, s32[32,8,128]{2,1,0:T(8,128)S(1)}) custom-call(s32[1,128]{1,0:T(1,128)S(1)} %reshape.9.packed, f32[2048,1024]{1,0:T(8,128)} %front.1, f32[2,512,512]{2,1,0:T(8,128)S(1)} %copy-done.1), custom_call_target="tpu_custom_call" | custom-call | tf_op jit(solution)/shard_map/front_update/pallas_call | solution.py:546
  244.0 0.0 copy-done
  244.0 6.0 %add_blocks.1 = (f32[48,128,128]{2,1,0:T(8,128)}, f32[2048,1024]{1,0:T(8,128)}, f32[256,1024]{1,0:T(8,128)}) custom-call(s32[32,8,128]{2,1,0:T(8,128)S(1)} %get-tuple-element.10.names, f32[48,128,128]{2,1,0:T(8,128)S(1)} %copy-done, f32[128,128,128]{2,1,0:T(8,128)S(1)} %get-tuple-element.11.arrived, f32[2048,1024]{1,0:T(8,128)S(1)} %get-tuple-element.12.updated, ...), custom_call_target="tpu_custom_call" | custom-call | tf_op jit(solution)/shard_map/add_blocks/pallas_call | solution.py:633
Async XLA Ops:
  1.5 1.6 copy-start.1
  3.1 240.9 %copy-start = (f32[48,128,128]{2,1,0:T(8,128)S(1)}, f32[48,128,128]{2,1,0:T(8,128)}, u32[]{:S(2)}) copy-start(f32[48,128,128]{2,1,0:T(8,128)} %parent.1) | copy-start | bytes 9437188
where the time goes:
time: 251 us; the launch traced here: 250 us
  Pallas kernels  247 us (98%)
    pallas_call x1, Pallas kernels, front_update(): pl.pallas_call(functools.partial(front_kernel, nrow, ncol, width, cap, br...  241 us
    pallas_call x1, Pallas kernels, add_blocks(): pl.pallas_call(functools.partial(add_kernel, lax.axis_size('col'), brows,...  6.01 us

commit v1 on v0

--- a/solution.py
+++ b/solution.py
@@ -294,8 +294,10 @@
             at = tile_rows(0, tile)
             ubuf[at, :] = acc[at, :]
 
-    def produce(p, i):
-        @pl.when(i == 0)
+    def produce(k, i):
+        p = k // mid
+
+        @pl.when((i == 0) & (k % mid == 0))
         def _():
             load_inv(p).wait()
             for q in range(width // 256):
@@ -310,12 +312,10 @@
         from_col = pl.ds(pl.multiple_of(p * width, width), width)
         both = jnp.concatenate([acc[tile_rows(h, tile), from_col] for h in range(2)], axis=0)
         a = stacked(both)
-        for q in range(mid):
-            out = jnp.dot(
-                a, istack[:, pl.ds(q * kc, kc)], preferred_element_type=jnp.float32
-            )
-            for h in range(2):
-                lbuf[p * mid + q, tile_rows(h, tile), :] = out[h * ts:(h + 1) * ts]
+        spot = pl.ds(pl.multiple_of(k % mid * kc, kc), kc)
+        out = jnp.dot(a, istack[:, spot], preferred_element_type=jnp.float32)
+        for h in range(2):
+            lbuf[k, tile_rows(h, tile), :] = out[h * ts:(h + 1) * ts]
 
     def step(t, carry):
         k = t // STEPS
@@ -330,13 +330,17 @@
         def _():
             load_rows.wait()
 
+        @pl.when((col == 0) & (k < nk) & (k % mid != 0))
+        def _():
+            produce(k, i)
+
         @pl.when(k > 0)
         def _():
             update(k - 1, i)
 
-        @pl.when((col == 0) & ((k == 0) | (k == mid)))
-        def _():
-            produce(k // mid, i)
+        @pl.when((col == 0) & (k < nk) & (k % mid == 0))
+        def _():
+            produce(k, i)
 
         @pl.when(k < nk)
         def _():

time: 251 us -> 252 us (level)
  no operation moved by 1% of the time
where the time goes in v1:
time: 252 us; the launch traced here: 249 us
  Pallas kernels  246 us (98%)
    pallas_call x1, Pallas kernels, front_update(): pl.pallas_call(functools.partial(front_kernel, nrow, ncol, width, cap, br...  240 us
    pallas_call x1, Pallas kernels, add_blocks(): pl.pallas_call(functools.partial(add_kernel, lax.axis_size('col'), brows,...  6.01 us

profile of v1, /device:TPU:15, one launch (start us, length us, event | category | flops | bytes accessed | tf_op | source)
XLA Modules:
  0.0 249.5 jit_solution(6919440845991277552)
XLA Ops:
  0.6 0.7 shift-left_add_fusion
  1.3 0.1 copy.9
  1.4 0.1 reshape.9.packed
  1.5 0.0 copy-start.1
  1.5 1.6 copy-done.1
  3.1 0.0 copy-start
  3.1 240.3 %front_update.1 = (f32[2048,1024]{1,0:T(8,128)S(1)}, f32[256,1024]{1,0:T(8,128)S(1)}, f32[128,128,128]{2,1,0:T(8,128)S(1)}, s32[32,8,128]{2,1,0:T(8,128)S(1)}) custom-call(s32[1,128]{1,0:T(1,128)S(1)} %reshape.9.packed, f32[2048,1024]{1,0:T(8,128)} %front.1, f32[2,512,512]{2,1,0:T(8,128)S(1)} %copy-done.1), custom_call_target="tpu_custom_call" | custom-call | tf_op jit(solution)/shard_map/front_update/pallas_call | solution.py:550
  243.4 0.0 copy-done
  243.4 6.0 %add_blocks.1 = (f32[48,128,128]{2,1,0:T(8,128)}, f32[2048,1024]{1,0:T(8,128)}, f32[256,1024]{1,0:T(8,128)}) custom-call(s32[32,8,128]{2,1,0:T(8,128)S(1)} %get-tuple-element.10.names, f32[48,128,128]{2,1,0:T(8,128)S(1)} %copy-done, f32[128,128,128]{2,1,0:T(8,128)S(1)} %get-tuple-element.11.arrived, f32[2048,1024]{1,0:T(8,128)S(1)} %get-tuple-element.12.updated, ...), custom_call_target="tpu_custom_call" | custom-call | tf_op jit(solution)/shard_map/add_blocks/pallas_call | solution.py:637
Async XLA Ops:
  1.5 1.6 copy-start.1
  3.1 240.3 %copy-start = (f32[48,128,128]{2,1,0:T(8,128)S(1)}, f32[48,128,128]{2,1,0:T(8,128)}, u32[]{:S(2)}) copy-start(f32[48,128,128]{2,1,0:T(8,128)} %parent.1) | copy-start | bytes 9437188
